TPU v7x, 128 devices: a whole 4x4x4 slice. The times are simulated.
128 devices in a mesh: lon: 8 (over x_hi, y), lat: 8 (over z, core), batch: 2 (over x_lo).
Axes of the slice: x: 4 (x_hi: 2, x_lo: 2; x = x_hi * 2 + x_lo), y: 4, z: 4, core: 2. Of those that a mesh axis runs over, the one named last changes fastest.
Arguments:
- state: bfloat16 [2, 21, 256, 4096], P('batch', None, 'lat', 'lon'), may hold values from -6 to 6
- forcing: bfloat16 [2, 96, 256, 4096], P('batch', None, 'lat', 'lon'), may hold values from -6 to 6
- land_mask: int32 [256, 4096], P('lat', 'lon'), may hold values 0 or 1
- partner: int32 [4096], P('lon'), may hold values from 0 to 4095, as said below
- cotangent: bfloat16 [2, 512, 128, 2048], P('batch', None, 'lat', 'lon'), may hold values from -6 to 6
- weight_state: bfloat16 [512, 336], replicated, may hold values from -0.125 to 0.125
- weight_force: bfloat16 [512, 1536], replicated, may hold values from -0.125 to 0.125
Outputs:
- grad_state: bfloat16 [2, 21, 256, 4096], P('batch', None, 'lat', 'lon')
- grad_forcing: bfloat16 [2, 96, 256, 4096], P('batch', None, 'lat', 'lon')
- grad_wstate: float32 [512, 336], P(('lat', 'batch'))
- grad_wforce: float32 [512, 1536], P(('lat', 'batch'))
Inputs may be any that keep to these rules, and one draw needn't show every extreme that they name: partner is an involution that maps the columns of the k-th block of 512 columns onto the columns of the block k-th from the other end, in an order drawn for each pair of blocks.
All inputs are finite; a program needn't handle non-finite values. No bound on the sum of `land_mask` on one device may be relied on, other than what follows from the above.
Results may differ from a plain program's by a relative error of at most 0.0011.
Values may be sent and summed in bfloat16 or wider, within the bound.
A program may use at most 256 MiB of HBM per device.

v0:
```python
import math
import jax
import jax.numpy as jnp
from jax import lax
from jax.sharding import PartitionSpec as P


def partner_2(block, axis, distance):
    count = lax.axis_size(axis)
    route = []
    for low in range(count):
        high = low | 1 << distance
        if high != low and high < count:
            route += [(low, high), (high, low)]
    return lax.ppermute(block, axis, route)


def with_halo(cells, sides, width):
    for axis, dim in sides:
        count = lax.axis_size(axis)
        head = lax.slice_in_dim(cells, 0, width, axis=dim)
        tail = lax.slice_in_dim(cells, cells.shape[dim] - width, cells.shape[dim], axis=dim)
        cells = jnp.concatenate(
            [
                lax.ppermute(tail, axis, [(i, (i + 1) % count) for i in range(count)]),
                cells,
                lax.ppermute(head, axis, [((i + 1) % count, i) for i in range(count)]),
            ],
            axis=dim,
        )
    return cells


def on_device(state, forcing, land_mask, partner, cotangent, weight_state, weight_force):
    state_ch = state.shape[1]
    channels = state_ch + forcing.shape[1]
    cell_rows = state.shape[2]
    cell_cols = state.shape[3]
    feat_width = cotangent.shape[1]
    tok_rows = cell_rows // 2
    tok_cols = cell_cols // 2
    lon_count = lax.axis_size("lon")
    lat_count = lax.axis_size("lat")
    batch_count = lax.axis_size("batch")
    lon_at = lax.axis_index("lon")
    lat_at = lax.axis_index("lat")
    at_top = lat_at == lat_count - 1
    at_bottom = lat_at == 0
    mirror_base = (lon_count - 1 - lon_at) * cell_cols
    local_col = partner - mirror_base
    bit_count = lon_count.bit_length() - 1
    bit_order = list(range(bit_count))
    masked = jnp.concatenate([state[0], forcing[0]], axis=0) * land_mask.astype(jnp.bfloat16)
    paired = masked[:, cell_rows - 1, :]
    for bit_pos in bit_order:
        paired = partner_2(paired, "lon", bit_pos)
    fold_row = jnp.take(paired, local_col, axis=1)
    row_ext = with_halo(masked, (("lat", 1),), 1)
    south_row = jnp.where(at_bottom, jnp.zeros_like(row_ext[:, 0, :]), row_ext[:, 0, :])
    north_row = jnp.where(at_top, fold_row, row_ext[:, cell_rows + 1, :])
    row_ext = jnp.concatenate(
        [south_row[:, None, :], row_ext[:, 1 : cell_rows + 1, :], north_row[:, None, :]], axis=1
    )
    padded = with_halo(row_ext, (("lon", 2),), 1)
    planes = [[padded[:, row_par::2, col_par::2] for col_par in range(2)] for row_par in range(2)]
    windows = []
    for row_off in range(4):
        for col_off in range(4):
            plane = planes[row_off % 2][col_off % 2]
            row_start = row_off // 2
            col_start = col_off // 2
            windows.append(
                plane[:, row_start : row_start + tok_rows, col_start : col_start + tok_cols]
            )
    grad_tokens = cotangent[0]
    scale = 1.0 / math.sqrt(
        cotangent.shape[0] * batch_count * tok_rows * lat_count * tok_cols * lon_count
    )
    share = feat_width // (lat_count * batch_count)
    terms = [
        lax.dot_general(
            grad_tokens, window, (((1, 2), (1, 2)), ((), ())), preferred_element_type=jnp.float32
        )
        for window in windows
    ]
    summed = lax.psum(
        jnp.stack(terms, axis=-1).reshape(grad_tokens.shape[0], channels * 16) * scale,
        ("lon", "lat", "batch"),
    )
    kernel_own = lax.dynamic_slice_in_dim(
        summed, lax.axis_index(("lat", "batch")) * share, share, 0
    )
    grad_ext = with_halo(cotangent[0], (("lat", 1), ("lon", 2)), 1)
    south_tok = jnp.where(at_bottom, jnp.zeros_like(grad_ext[:, :1, :]), grad_ext[:, :1, :])
    north_tok = jnp.where(at_top, jnp.zeros_like(grad_ext[:, -1:, :]), grad_ext[:, -1:, :])
    grad_ext = jnp.concatenate([south_tok, grad_ext[:, 1 : tok_rows + 1, :], north_tok], axis=1)
    weights = jnp.concatenate([weight_state, weight_force], axis=1)
    spread_all = lax.dot_general(
        weights, grad_ext, (((0,), (0,)), ((), ())), preferred_element_type=jnp.float32
    )
    spread_all = spread_all.reshape(channels, 4, 4, tok_rows + 2, tok_cols + 2)
    parity_terms = (((1, 1), (3, 0)), ((0, 2), (2, 1)))
    fold_cols = []
    for col_par in range(2):
        acc_fold = jnp.zeros((channels, tok_cols), jnp.float32)
        for col_off, col_start in parity_terms[col_par]:
            acc_fold = (
                acc_fold + spread_all[:, 3, col_off, tok_rows, col_start : col_start + tok_cols]
            )
        fold_cols.append(acc_fold)
    fold_part = jnp.stack(fold_cols, axis=-1).reshape(channels, cell_cols)
    arrived = jnp.zeros((channels, cell_cols), jnp.float32).at[:, local_col].set(fold_part)
    for bit_pos in bit_order:
        arrived = partner_2(arrived.astype(jnp.bfloat16), "lon", bit_pos).astype(arrived.dtype)
    arrived = jnp.where(at_top, arrived, jnp.zeros_like(arrived))
    mask_float = land_mask.astype(jnp.float32)
    row_blocks = []
    for row_par in range(2):
        col_blocks = []
        for col_par in range(2):
            acc_cells = jnp.zeros((channels, tok_rows, tok_cols), jnp.float32)
            for row_off, row_start in parity_terms[row_par]:
                for col_off, col_start in parity_terms[col_par]:
                    acc_cells = (
                        acc_cells
                        + spread_all[
                            :,
                            row_off,
                            col_off,
                            row_start : row_start + tok_rows,
                            col_start : col_start + tok_cols,
                        ]
                    )
            if row_par == 1:
                acc_cells = acc_cells.at[:, tok_rows - 1, :].add(arrived[:, col_par::2])
            mask_plane = mask_float[row_par::2, col_par::2]
            col_blocks.append((acc_cells * mask_plane).astype(jnp.bfloat16))
        row_blocks.append(jnp.stack(col_blocks, axis=-1))
    result = jnp.stack(row_blocks, axis=2).reshape(channels, cell_rows, cell_cols)
    return (
        result[None, :state_ch],
        result[None, state_ch:],
        kernel_own[:, : state_ch * 16],
        kernel_own[:, state_ch * 16 :],
    )


def solution(mesh):
    in_specs = (
        P("batch", None, "lat", "lon"),
        P("batch", None, "lat", "lon"),
        P("lat", "lon"),
        P("lon"),
        P("batch", None, "lat", "lon"),
        P(),
        P(),
    )
    out_specs = (
        P("batch", None, "lat", "lon"),
        P("batch", None, "lat", "lon"),
        P(("lat", "batch"), None),
        P(("lat", "batch"), None),
    )
    return jax.shard_map(
        on_device, mesh=mesh, in_specs=in_specs, out_specs=out_specs, check_vma=False
    )
```

profile of v0, /device:TPU:1, one launch (start us, length us, event | category | flops | bytes accessed | tf_op | source)
XLA Modules:
  0.0 742.1 jit_solution(12922439610931023367)
XLA Ops:
  7.2 7.8 %copy.200 = bf16[1,512,16,256]{1,3,2,0:T(8,128)(2,1)} copy(bf16[1,512,16,256]{3,2,1,0:T(8,128)(2,1)} %param.15) | data formatting | bytes 8388608 | tf_op args[4]
  35.5 7.6 %copy.251 = bf16[512,16,256]{0,2,1:T(8,128)(2,1)} copy(bf16[512,16,256]{2,1,0:T(8,128)(2,1)} %bitcast.187) | data formatting | bytes 8388608 | tf_op jit(solution)/shard_map/squeeze | solution.py:93
  55.9 6.6 pad_maximum_fusion.1
  64.6 22.9 %fusion = f32[1872,18,258]{2,0,1:T(8,128)} fusion(bf16[512,1,258]{0,2,1:T(8,128)(2,1)} %get-tuple-element.65, bf16[512,16,258]{0,2,1:T(8,128)(2,1)S(1)} %slice.297, bf16[512,1,258]{0,2,1:T(8,128)(2,1)S(1)} %get-tuple-element.64, bf16[512,1536]{0,1:T(8,128)(2,1)} %copy.199, bf16[512,336]{0,1:T(8,128)(2,1)} %param.16), kind=kOutput, calls=%fused_computation.4 | convolution fusion | flops 8920313856 | bytes 41446656 | tf_op jit(solution)/shard_map/dot_general | solution.py:98
  87.6 58.6 %reshape.251 = f32[117,4,4,18,258]{4,2,1,0,3:T(4,128)} reshape(f32[1872,18,258]{2,0,1:T(8,128)} %fusion) | data formatting | bytes 69548544 | tf_op jit(solution)/shard_map/reshape | solution.py:101
  146.2 72.5 %fusion.36 = (f32[117,1,1,16,256]{4,2,1,0,3:T(1,128)}, f32[117,1,1,16,256]{4,2,1,0,3:T(1,128)}, f32[117,1,1,16,256]{4,2,1,0,3:T(1,128)}, f32[117,1,1,16,256]{4,2...) fusion(f32[117,4,4,18,258]{4,2,1,0,3:T(4,128)} %reshape.251), kind=kLoop, calls=%fused_computation.92 | loop fusion | bytes 61341696 | tf_op jit(solution)/shard_map/slice | solution.py:126
  235.3 6.1 copy.303
  241.4 6.1 copy.304
  247.5 6.1 copy.302
  271.9 7.4 fusion.6
  289.9 6.1 copy.307
  296.0 6.1 copy.308
  317.0 6.2 copy.314
  326.8 6.2 copy.311
  337.8 7.6 %pad_maximum_fusion = bf16[117,34,514]{2,0,1:T(8,128)(2,1)} fusion(bf16[117,34,1]{2,0,1:T(8,128)(2,1)S(1)} %copy.229, bf16[117,1,512]{2,0,1:T(8,128)(2,1)S(1)} %fusion.32, bf16[117,32,512]{2,0,1:T(8,128)(2,1)} %copy-done.3, bf16[117,1,512]{2,0,1:T(8,128)(2,1)S(1)} %broadcast_select_fusion, bf16[117,34,1]{2,0,1:T(8,128)(2,1)S(1)} %copy.228), kind=kLoop, calls=%fused_computation.2 | loop fusion | flops 20446920 | bytes 8178768 | tf_op jit(solution)/shard_map/concatenate | solution.py:23
  345.4 42.5 %slice.271 = bf16[117,17,257]{2,0,1:T(8,128)(2,1)S(1)} slice(bf16[117,34,514]{2,0,1:T(8,128)(2,1)} %pad_maximum_fusion), slice={[0:117:1], [0:34:2], [0:514:2]} | slice | bytes 2044692 | tf_op jit(solution)/shard_map/slice | solution.py:65
  388.0 42.9 %slice.273 = bf16[117,17,257]{2,0,1:T(8,128)(2,1)S(1)} slice(bf16[117,34,514]{2,0,1:T(8,128)(2,1)} %pad_maximum_fusion), slice={[0:117:1], [0:34:2], [1:514:2]} | slice | bytes 2044692 | tf_op jit(solution)/shard_map/slice | solution.py:65
  438.4 41.6 %slice.277 = bf16[117,17,257]{2,0,1:T(8,128)(2,1)} slice(bf16[117,34,514]{2,0,1:T(8,128)(2,1)} %pad_maximum_fusion), slice={[0:117:1], [1:34:2], [0:514:2]} | slice | bytes 2044692 | tf_op jit(solution)/shard_map/slice | solution.py:65
  480.0 43.0 %slice.279 = bf16[117,17,257]{2,0,1:T(8,128)(2,1)S(1)} slice(bf16[117,34,514]{2,0,1:T(8,128)(2,1)} %pad_maximum_fusion), slice={[0:117:1], [1:34:2], [1:514:2]} | slice | bytes 2044692 | tf_op jit(solution)/shard_map/slice | solution.py:65
  542.1 28.3 %stack.103 = f32[512,117,16]{0,2,1:T(8,128)} concatenate(f32[512,117,1]{0,2,1:T(1,128)S(1)} %stack.87, f32[512,117,1]{0,2,1:T(1,128)S(1)} %stack.88, f32[512,117,1]{0,2,1:T(1,128)S(1)} %stack.89, f32[512,117,1]{0,2,1:T(1,128)S(1)} %stack.90, f32[512,117,1]{0,2,1:T(1,128)S(1)} %stack.91, f32[512,117,1]{0,2,1:T(1,128)S(1)} %stack.92, f32[512,117,1]{0,2,1:T(1,128)S(1)} %stack.93, ...), dimensions={2} | concatenate | bytes 7667712 | tf_op jit(solution)/shard_map/stack | solution.py:87
  598.2 8.6 %copy.220 = bf16[21,16,2,256,2]{0,4,3,2,1:T(2,128)(2,1)} copy(bf16[21,16,2,256,2]{0,3,1,4,2:T(8,128)(2,1)} %slice_maximum_fusion) | data formatting | bytes 1376256 | tf_op jit(solution)/shard_map/slice | solution.py:141
  616.7 8.6 %copy.221 = bf16[96,16,2,256,2]{0,4,3,2,1:T(2,128)(2,1)} copy(bf16[96,16,2,256,2]{0,3,1,4,2:T(8,128)(2,1)} %pad_maximum_fusion.2) | data formatting | bytes 6291456 | tf_op jit(solution)/shard_map/slice | solution.py:142
  625.3 7.4 copy.247
  632.7 98.3 %all-reduce.2.cloned.1.call-done = f32[512,1872]{0,1:T(8,128)} async-done(((f32[512,1872]{0,1:T(8,128)}), f32[512,1872]{0,1:T(8,128)}) %all-reduce.2.cloned.1.call-update) | async-done | bytes 3833872 | tf_op jit(solution)/shard_map/psum | solution.py:86
  (166 shorter events, 172.1 us)
Async XLA Ops:
  7.2 12.7 %copy-start.21 = (s32[32,512]{1,0:T(8,128)S(1)}, s32[32,512]{1,0:T(8,128)}, u32[]{:S(2)}) copy-start(s32[32,512]{1,0:T(8,128)} %param.13) | copy-start | bytes 196612
  7.2 723.8 %all-reduce.2.cloned.1.call-start = ((), (), s32[]{:S(2)}) async-start(), calls=%async_computation | async-start | bytes 7667712 | tf_op jit(solution)/shard_map/psum | solution.py:86
  7.2 12.7 %copy-start.13 = (bf16[1,96,32,512]{3,2,1,0:T(8,128)(2,1)S(1)}, bf16[1,96,32,512]{3,2,1,0:T(8,128)(2,1)}, u32[]{:S(2)}) copy-start(bf16[1,96,32,512]{3,2,1,0:T(8,128)(2,1)} %param.12) | copy-start | bytes 9437188
  16.8 28.8 %collective-permute-start.1 = (bf16[512,1,256]{0,2,1:T(8,128)(2,1)}, bf16[512,1,256]{0,2,1:T(8,128)(2,1)S(1)}, u32[]{:S(2)}, u32[]{:S(2)}) collective-permute-start(bf16[512,1,256]{0,2,1:T(8,128)(2,1)} %get-tuple-element.69), channel_id=1, source_target_pairs={{2,0},{4,2},{6,4},{8,6},{10,8},{12,10},{14,12},{0,14},{3,1},{5,3},... | collective-permute-start | bytes 786440 | tf_op jit(solution)/shard_map/ppermute | solution.py:27
  18.3 27.4 %collective-permute-start = (bf16[512,1,256]{0,2,1:T(8,128)(2,1)}, bf16[512,1,256]{0,2,1:T(8,128)(2,1)}, u32[]{:S(2)}, u32[]{:S(2)}) collective-permute-start(bf16[512,1,256]{0,2,1:T(8,128)(2,1)} %get-tuple-element.68), channel_id=1, source_target_pairs={{0,2},{2,4},{4,6},{6,8},{8,10},{10,12},{12,14},{14,0},{1,3},{3,5},... | collective-permute-start | bytes 786440 | tf_op jit(solution)/shard_map/ppermute | solution.py:25
  22.1 8.1 %copy-start.22 = (s32[512]{0:T(512)S(1)}, s32[512]{0:T(512)}, u32[]{:S(2)}) copy-start(s32[512]{0:T(512)} %param.14) | copy-start | bytes 6148
  22.1 11.8 %copy-start.14 = (bf16[512,1536]{1,0:T(8,128)(2,1)S(1)}, bf16[512,1536]{1,0:T(8,128)(2,1)}, u32[]{:S(2)}) copy-start(bf16[512,1536]{1,0:T(8,128)(2,1)} %param.17) | copy-start | bytes 4718596
  26.9 277.8 %collective-permute-start.11 = (bf16[117,1,512]{2,0,1:T(8,128)(2,1)}, bf16[117,1,512]{2,0,1:T(8,128)(2,1)}, u32[]{:S(2)}, u32[]{:S(2)}) collective-permute-start(bf16[117,1,512]{2,0,1:T(8,128)(2,1)} %get-tuple-element.74), channel_id=1, source_target_pairs={{2,0},{4,2},{6,4},{8,6},{10,8},{12,10},{14,12},{0,14},{3,1},{5,3},... | collective-permute-start | bytes 359432 | tf_op jit(solution)/shard_map/ppermute | solution.py:27
  28.8 14.2 %collective-permute-start.8 = (bf16[117,512]{1,0:T(8,128)(2,1)S(1)}, bf16[117,512]{1,0:T(8,128)(2,1)S(1)}, u32[]{:S(2)}, u32[]{:S(2)}) collective-permute-start(bf16[117,512]{1,0:T(8,128)(2,1)S(1)} %get-tuple-element.73), channel_id=1, source_target_pairs={{0,16},{16,0},{32,48},{48,32},{64,80},{80,64},{96,112},{112,96},{1... | collective-permute-start | bytes 359432 | tf_op jit(solution)/shard_map/ppermute | solution.py:15
  30.1 19.4 %collective-permute-start.7 = (bf16[117,1,512]{2,0,1:T(8,128)(2,1)S(1)}, bf16[117,1,512]{2,0,1:T(8,128)(2,1)S(1)}, u32[]{:S(2)}, u32[]{:S(2)}) collective-permute-start(bf16[117,1,512]{2,0,1:T(8,128)(2,1)S(1)} %get-tuple-element.72), channel_id=1, source_target_pairs={{0,2},{2,4},{4,6},{6,8},{8,10},{10,12},{12,14},{14,0},{1,3},{3,5},... | collective-permute-start | bytes 359432 | tf_op jit(solution)/shard_map/ppermute | solution.py:25
  43.0 12.9 %copy-start.2 = (bf16[1,512,16,256]{1,3,2,0:T(8,128)(2,1)S(1)}, bf16[1,512,16,256]{1,3,2,0:T(8,128)(2,1)}, u32[]{:S(2)}) copy-start(bf16[1,512,16,256]{1,3,2,0:T(8,128)(2,1)} %copy.200) | copy-start | bytes 12582916
  43.0 6.5 collective-permute-start.9
  46.7 4.7 collective-permute-start.3
  49.5 6.4 collective-permute-start.2
  49.5 252.6 %collective-permute-start.10 = (bf16[117,512]{1,0:T(8,128)(2,1)}, bf16[117,512]{1,0:T(8,128)(2,1)}, u32[]{:S(2)}, u32[]{:S(2)}) collective-permute-start(bf16[117,512]{1,0:T(8,128)(2,1)} %collective-permute-done.9), channel_id=1, source_target_pairs={{0,64},{64,0},{16,80},{80,16},{32,96},{96,32},{48,112},{112,48},{1... | collective-permute-start | bytes 359432 | tf_op jit(solution)/shard_map/ppermute | solution.py:15
  224.5 350.8 %collective-permute-start.4 = (bf16[117,512]{0,1:T(8,128)(2,1)}, bf16[117,512]{0,1:T(8,128)(2,1)}, u32[]{:S(2)}, u32[]{:S(2)}) collective-permute-start(bf16[117,512]{0,1:T(8,128)(2,1)} %convert_element_type.45), channel_id=1, source_target_pairs={{0,16},{16,0},{32,48},{48,32},{64,80},{80,64},{96,112},{112,96},{1... | collective-permute-start | bytes 359432 | tf_op jit(solution)/shard_map/ppermute | solution.py:15
  310.2 26.5 %collective-permute-start.13 = (bf16[117,34,1]{0,1,2:T(8,128)(2,1)S(1)}, bf16[117,34,1]{0,1,2:T(8,128)(2,1)S(1)}, u32[]{:S(2)}, u32[]{:S(2)}) collective-permute-start(bf16[117,34,1]{0,1,2:T(8,128)(2,1)S(1)} %copy.227), channel_id=1, source_target_pairs={{16,0},{32,16},{48,32},{64,48},{80,64},{96,80},{112,96},{0,112},{1... | collective-permute-start | bytes 23876 | tf_op jit(solution)/shard_map/ppermute | solution.py:27
  311.2 26.1 %collective-permute-start.12 = (bf16[117,34,1]{0,1,2:T(8,128)(2,1)S(1)}, bf16[117,34,1]{0,1,2:T(8,128)(2,1)S(1)}, u32[]{:S(2)}, u32[]{:S(2)}) collective-permute-start(bf16[117,34,1]{0,1,2:T(8,128)(2,1)S(1)} %copy.226), channel_id=1, source_target_pairs={{0,16},{16,32},{32,48},{48,64},{64,80},{80,96},{96,112},{112,0},{1... | collective-permute-start | bytes 23876 | tf_op jit(solution)/shard_map/ppermute | solution.py:25
  388.0 46.7 %copy-start.4 = (bf16[117,17,257]{2,0,1:T(8,128)(2,1)}, bf16[117,17,257]{2,0,1:T(8,128)(2,1)S(1)}, u32[]{:S(2)}) copy-start(bf16[117,17,257]{2,0,1:T(8,128)(2,1)S(1)} %slice.271) | copy-start | bytes 3067042
  575.3 7.3 copy-start.11
  575.3 7.0 collective-permute-start.5
  582.3 5.3 collective-permute-start.6
  582.5 8.5 %copy-start.19 = (f32[16,256]{1,0:T(8,128)S(1)}, f32[16,256]{1,0:T(8,128)}, u32[]{:S(2)}) copy-start(f32[16,256]{1,0:T(8,128)} %slice.257) | copy-start | bytes 49156
  582.5 8.5 %copy-start.20 = (f32[16,256]{1,0:T(8,128)S(1)}, f32[16,256]{1,0:T(8,128)}, u32[]{:S(2)}) copy-start(f32[16,256]{1,0:T(8,128)} %slice.264) | copy-start | bytes 49156
  (14 other events, 40.8 us)
Sparse Core Ops, SparseCore 0:
  575.4 155.5 all-reduce.1
where the time goes:
time: 754 us; the launch traced here: 742 us
  local copies, waits for them, and re-layouts  495 us (66%)
  waiting for transfers between devices  107 us (14%)
  other arithmetic  63.1 us (8%)
  matrix products  43.5 us (6%)
  starting transfers between devices  17.7 us (2%)
  between operations  14.9 us (2%)
    slice x4, local copies, waits for them, and re-layouts, on_device(): padded[:, row_par::2, col_par::2]  170 us
    unnamed x70, local copies, waits for them, and re-layouts  120 us
    psum x1, waiting for transfers between devices, on_device(): lax.psum(jnp.stack(terms, axis=-1).reshape(grad_tokens.shape[0], channels...  98.3 us
    slice x1, local copies, waits for them, and re-layouts, on_device(): spread_all[:, row_off, col_off, row_start:row_start + tok_rows, col_start...  72.5 us
    reshape x1, local copies, waits for them, and re-layouts, on_device(): spread_all = spread_all.reshape(channels, 4, 4, tok_rows + 2, tok_cols + 2)  58.6 us
    another operation x17, local copies, waits for them, and re-layouts, on_device(): jnp.stack(terms, axis=-1).reshape(grad_tokens.shape[0], channels * 16)  32.4 us
    dot_general x1, matrix products, on_device(): lax.dot_general(weights, grad_ext, (((0,), (0,)), ((), ())), preferred_el...  22.9 us
    dot_general x16, matrix products, on_device(): lax.dot_general(grad_tokens, window, (((1, 2), (1, 2)), ((), ())), prefer...  20.6 us
  transfers between devices with their start and end apart: 15, of which 3 were waited for; matrix products, arithmetic and copies ran while one was open for 79% of the time, Pallas kernels for 0%

commit v1 on v0

--- a/solution.py
+++ b/solution.py
@@ -83,10 +83,8 @@
         )
         for window in windows
     ]
-    summed = lax.psum(
-        jnp.stack(terms, axis=-1).reshape(grad_tokens.shape[0], channels * 16) * scale,
-        ("lon", "lat", "batch"),
-    )
+    w_in = jnp.stack(terms, axis=-1).reshape(grad_tokens.shape[0], channels * 16) * scale
+    summed = lax.psum(lax.psum(w_in, "lon"), ("lat", "batch"))
     kernel_own = lax.dynamic_slice_in_dim(
         summed, lax.axis_index(("lat", "batch")) * share, share, 0
     )

time: 754 us -> 709 us (0.940)
  waiting for transfers between devices: 107 us -> 59.8 us
    psum x1 -> x2, waiting for transfers between devices: 98.3 us -> 49.1 us  [on_device(): summed = lax.psum(lax.psum(w_in, 'lon'), ('lat', 'batch'))]
  transfers between devices with their start and end apart: 15 -> 16, of which waited for: 3 -> 4; matrix products, arithmetic and copies ran while one was open for 79% -> 49% of each run, Pallas kernels for 0% -> 0%
where the time goes in v1:
time: 709 us; the launch traced here: 697 us
  local copies, waits for them, and re-layouts  500 us (71%)
  waiting for transfers between devices  59.8 us (8%)
  other arithmetic  57.5 us (8%)
  matrix products  44.2 us (6%)
  starting transfers between devices  20.1 us (3%)
  between operations  14.9 us (2%)
    slice x4, local copies, waits for them, and re-layouts, on_device(): padded[:, row_par::2, col_par::2]  170 us
    unnamed x70, local copies, waits for them, and re-layouts  126 us
    slice x1, local copies, waits for them, and re-layouts, on_device(): spread_all[:, row_off, col_off, row_start:row_start + tok_rows, col_start...  72.7 us
    reshape x1, local copies, waits for them, and re-layouts, on_device(): spread_all = spread_all.reshape(channels, 4, 4, tok_rows + 2, tok_cols + 2)  58.6 us
    psum x2, waiting for transfers between devices, on_device(): summed = lax.psum(lax.psum(w_in, 'lon'), ('lat', 'batch'))  49.1 us
    another operation x17, local copies, waits for them, and re-layouts, on_device(): jnp.stack(terms, axis=-1).reshape(grad_tokens.shape[0], channels * 16)  32.4 us
    dot_general x1, matrix products, on_device(): lax.dot_general(weights, grad_ext, (((0,), (0,)), ((), ())), preferred_el...  23.6 us
    dot_general x16, matrix products, on_device(): lax.dot_general(grad_tokens, window, (((1, 2), (1, 2)), ((), ())), prefer...  20.6 us
  transfers between devices with their start and end apart: 16, of which 4 were waited for; matrix products, arithmetic and copies ran while one was open for 49% of the time, Pallas kernels for 0%

profile of v1, /device:TPU:1, one launch (start us, length us, event | category | flops | bytes accessed | tf_op | source)
XLA Modules:
  0.0 696.8 jit_solution(5908889463700152482)
XLA Ops:
  7.2 7.8 %copy.200 = bf16[1,512,16,256]{1,3,2,0:T(8,128)(2,1)} copy(bf16[1,512,16,256]{3,2,1,0:T(8,128)(2,1)} %param.15) | data formatting | bytes 8388608 | tf_op args[4]
  34.8 7.6 %copy.251 = bf16[512,16,256]{0,2,1:T(8,128)(2,1)} copy(bf16[512,16,256]{2,1,0:T(8,128)(2,1)} %bitcast.187) | data formatting | bytes 8388608 | tf_op jit(solution)/shard_map/squeeze | solution.py:91
  55.3 6.6 pad_maximum_fusion.1
  71.5 23.6 %fusion = f32[1872,18,258]{2,0,1:T(8,128)} fusion(bf16[512,1,258]{0,2,1:T(8,128)(2,1)S(1)} %get-tuple-element.65, bf16[512,16,258]{0,2,1:T(8,128)(2,1)} %slice.297, bf16[512,1,258]{0,2,1:T(8,128)(2,1)S(1)} %get-tuple-element.64, bf16[512,1536]{0,1:T(8,128)(2,1)} %copy.199, bf16[512,336]{0,1:T(8,128)(2,1)S(1)} %copy-done.22), kind=kOutput, calls=%fused_computation.4 | convolution fusion | flops 8920313856 | bytes 41446656 | tf_op jit(solution)/shard_map/dot_general | solution.py:96
  95.2 58.6 %reshape.251 = f32[117,4,4,18,258]{4,2,1,0,3:T(4,128)} reshape(f32[1872,18,258]{2,0,1:T(8,128)} %fusion) | data formatting | bytes 69548544 | tf_op jit(solution)/shard_map/reshape | solution.py:99
  154.9 7.6 %pad_maximum_fusion = bf16[117,34,514]{2,0,1:T(8,128)(2,1)} fusion(bf16[117,34,1]{2,0,1:T(8,128)(2,1)S(1)} %copy.229, bf16[117,1,512]{2,0,1:T(8,128)(2,1)S(1)} %fusion.32, bf16[117,32,512]{2,0,1:T(8,128)(2,1)} %copy-done.3, bf16[117,1,512]{2,0,1:T(8,128)(2,1)S(1)} %broadcast_select_fusion, bf16[117,34,1]{2,0,1:T(8,128)(2,1)S(1)} %copy.228), kind=kLoop, calls=%fused_computation.2 | loop fusion | flops 20446920 | bytes 8178768 | tf_op jit(solution)/shard_map/concatenate | solution.py:23
  162.6 42.5 %slice.271 = bf16[117,17,257]{2,0,1:T(8,128)(2,1)S(1)} slice(bf16[117,34,514]{2,0,1:T(8,128)(2,1)} %pad_maximum_fusion), slice={[0:117:1], [0:34:2], [0:514:2]} | slice | bytes 2044692 | tf_op jit(solution)/shard_map/slice | solution.py:65
  205.1 42.9 %slice.273 = bf16[117,17,257]{2,0,1:T(8,128)(2,1)S(1)} slice(bf16[117,34,514]{2,0,1:T(8,128)(2,1)} %pad_maximum_fusion), slice={[0:117:1], [0:34:2], [1:514:2]} | slice | bytes 2044692 | tf_op jit(solution)/shard_map/slice | solution.py:65
  255.5 41.6 %slice.277 = bf16[117,17,257]{2,0,1:T(8,128)(2,1)} slice(bf16[117,34,514]{2,0,1:T(8,128)(2,1)} %pad_maximum_fusion), slice={[0:117:1], [1:34:2], [0:514:2]} | slice | bytes 2044692 | tf_op jit(solution)/shard_map/slice | solution.py:65
  297.1 43.0 %slice.279 = bf16[117,17,257]{2,0,1:T(8,128)(2,1)S(1)} slice(bf16[117,34,514]{2,0,1:T(8,128)(2,1)} %pad_maximum_fusion), slice={[0:117:1], [1:34:2], [1:514:2]} | slice | bytes 2044692 | tf_op jit(solution)/shard_map/slice | solution.py:65
  359.2 28.3 %stack.103 = f32[512,117,16]{0,2,1:T(8,128)} concatenate(f32[512,117,1]{0,2,1:T(1,128)S(1)} %stack.87, f32[512,117,1]{0,2,1:T(1,128)S(1)} %stack.88, f32[512,117,1]{0,2,1:T(1,128)S(1)} %stack.89, f32[512,117,1]{0,2,1:T(1,128)S(1)} %stack.90, f32[512,117,1]{0,2,1:T(1,128)S(1)} %stack.91, f32[512,117,1]{0,2,1:T(1,128)S(1)} %stack.92, f32[512,117,1]{0,2,1:T(1,128)S(1)} %stack.93, ...), dimensions={2} | concatenate | bytes 7667712 | tf_op jit(solution)/shard_map/stack | solution.py:86
  392.4 72.7 %fusion.36 = (f32[117,1,1,16,256]{4,2,1,0,3:T(1,128)}, f32[117,1,1,16,256]{4,2,1,0,3:T(1,128)}, f32[117,1,1,16,256]{4,2,1,0,3:T(1,128)}, f32[117,1,1,16,256]{4,2...) fusion(f32[117,4,4,18,258]{4,2,1,0,3:T(4,128)} %reshape.251), kind=kLoop, calls=%fused_computation.92 | loop fusion | bytes 61341696 | tf_op jit(solution)/shard_map/slice | solution.py:124
  465.1 33.5 %all-reduce.3.cloned.1.call-done = f32[512,1872]{0,1:T(8,128)} async-done(((f32[512,1872]{0,1:T(8,128)}), f32[512,1872]{0,1:T(8,128)}) %all-reduce.3.cloned.1.call-update) | async-done | bytes 3833872 | tf_op jit(solution)/shard_map/psum | solution.py:87
  506.1 6.1 copy.309
  518.3 6.1 copy.308
  526.7 6.5 copy.306
  563.8 6.1 copy.299
  576.0 7.8 %fusion.6 = (bf16[117,16,256,1]{0,2,1,3:T(8,128)(2,1)S(1)}, bf16[117,16,256,1]{0,2,1,3:T(8,128)(2,1)}) fusion(f32[117,1,1,16,256]{0,4,3,2,1:T(8,128)} %copy.306, f32[117,1,1,16,256]{0,4,3,2,1:T(8,128)} %copy.305, f32[117,1,1,16,256]{0,4,3,2,1:T(8,128)} %copy.303, f32[117,1,1,16,256]{0,4,3,2,1:T(8,128)} %copy.304, f32[16,256]{1,0:T(8,128)S(1)} %slice.246, ...), kind=kLoop, calls=%fused_computation.17 | loop fusion | flops 4792320 | bytes 17285120 | tf_op jit(solution)/shard_map/convert_element_type | solution.py:135
  602.9 6.1 copy.312
  618.9 6.2 collective-permute-done.6
  635.6 8.6 %copy.220 = bf16[21,16,2,256,2]{0,4,3,2,1:T(2,128)(2,1)} copy(bf16[21,16,2,256,2]{0,3,1,4,2:T(8,128)(2,1)} %slice_maximum_fusion) | data formatting | bytes 1376256 | tf_op jit(solution)/shard_map/slice | solution.py:139
  654.1 8.6 %copy.221 = bf16[96,16,2,256,2]{0,4,3,2,1:T(2,128)(2,1)} copy(bf16[96,16,2,256,2]{0,3,1,4,2:T(8,128)(2,1)} %pad_maximum_fusion.2) | data formatting | bytes 6291456 | tf_op jit(solution)/shard_map/slice | solution.py:140
  662.7 7.4 %copy.247 = bf16[1,96,32,512]{3,2,1,0:T(8,128)(2,1)} copy(bf16[1,96,32,512]{1,3,2,0:T(8,128)(2,1)} %bitcast.186) | data formatting | bytes 6291456
  670.1 15.7 %all-reduce.5.cloned.1.call-done = f32[512,1872]{0,1:T(8,128)} async-done(((f32[512,1872]{0,1:T(8,128)}), f32[512,1872]{0,1:T(8,128)}) %all-reduce.5.cloned.1.call-update) | async-done | bytes 3833872 | tf_op jit(solution)/shard_map/psum | solution.py:87
  (169 shorter events, 180.4 us)
Async XLA Ops:
  7.2 12.7 %copy-start.20 = (s32[32,512]{1,0:T(8,128)S(1)}, s32[32,512]{1,0:T(8,128)}, u32[]{:S(2)}) copy-start(s32[32,512]{1,0:T(8,128)} %param.13) | copy-start | bytes 196612
  7.2 491.4 %all-reduce.3.cloned.1.call-start = ((), (), s32[]{:S(2)}) async-start(), calls=%async_computation | async-start | bytes 7667712 | tf_op jit(solution)/shard_map/psum | solution.py:87
  7.2 12.7 %copy-start.12 = (bf16[1,96,32,512]{3,2,1,0:T(8,128)(2,1)S(1)}, bf16[1,96,32,512]{3,2,1,0:T(8,128)(2,1)}, u32[]{:S(2)}) copy-start(bf16[1,96,32,512]{3,2,1,0:T(8,128)(2,1)} %param.12) | copy-start | bytes 9437188
  16.8 28.2 %collective-permute-start.1 = (bf16[512,1,256]{0,2,1:T(8,128)(2,1)}, bf16[512,1,256]{0,2,1:T(8,128)(2,1)S(1)}, u32[]{:S(2)}, u32[]{:S(2)}) collective-permute-start(bf16[512,1,256]{0,2,1:T(8,128)(2,1)} %get-tuple-element.69), channel_id=1, source_target_pairs={{2,0},{4,2},{6,4},{8,6},{10,8},{12,10},{14,12},{0,14},{3,1},{5,3},... | collective-permute-start | bytes 786440 | tf_op jit(solution)/shard_map/ppermute | solution.py:27
  18.3 26.8 %collective-permute-start = (bf16[512,1,256]{0,2,1:T(8,128)(2,1)}, bf16[512,1,256]{0,2,1:T(8,128)(2,1)}, u32[]{:S(2)}, u32[]{:S(2)}) collective-permute-start(bf16[512,1,256]{0,2,1:T(8,128)(2,1)} %get-tuple-element.68), channel_id=1, source_target_pairs={{0,2},{2,4},{4,6},{6,8},{8,10},{10,12},{12,14},{14,0},{1,3},{3,5},... | collective-permute-start | bytes 786440 | tf_op jit(solution)/shard_map/ppermute | solution.py:25
  22.1 11.2 %copy-start.13 = (bf16[512,1536]{1,0:T(8,128)(2,1)S(1)}, bf16[512,1536]{1,0:T(8,128)(2,1)}, u32[]{:S(2)}) copy-start(bf16[512,1536]{1,0:T(8,128)(2,1)} %param.17) | copy-start | bytes 4718596
  26.2 40.8 %collective-permute-start.11 = (bf16[117,1,512]{2,0,1:T(8,128)(2,1)S(1)}, bf16[117,1,512]{2,0,1:T(8,128)(2,1)S(1)}, u32[]{:S(2)}, u32[]{:S(2)}) collective-permute-start(bf16[117,1,512]{2,0,1:T(8,128)(2,1)S(1)} %get-tuple-element.74), channel_id=1, source_target_pairs={{2,0},{4,2},{6,4},{8,6},{10,8},{12,10},{14,12},{0,14},{3,1},{5,3},... | collective-permute-start | bytes 359432 | tf_op jit(solution)/shard_map/ppermute | solution.py:27
  28.2 14.2 %collective-permute-start.8 = (bf16[117,512]{1,0:T(8,128)(2,1)S(1)}, bf16[117,512]{1,0:T(8,128)(2,1)S(1)}, u32[]{:S(2)}, u32[]{:S(2)}) collective-permute-start(bf16[117,512]{1,0:T(8,128)(2,1)S(1)} %get-tuple-element.73), channel_id=1, source_target_pairs={{0,16},{16,0},{32,48},{48,32},{64,80},{80,64},{96,112},{112,96},{1... | collective-permute-start | bytes 359432 | tf_op jit(solution)/shard_map/ppermute | solution.py:15
  29.5 19.4 %collective-permute-start.7 = (bf16[117,1,512]{2,0,1:T(8,128)(2,1)S(1)}, bf16[117,1,512]{2,0,1:T(8,128)(2,1)S(1)}, u32[]{:S(2)}, u32[]{:S(2)}) collective-permute-start(bf16[117,1,512]{2,0,1:T(8,128)(2,1)S(1)} %get-tuple-element.72), channel_id=1, source_target_pairs={{0,2},{2,4},{4,6},{6,8},{8,10},{10,12},{12,14},{14,0},{1,3},{3,5},... | collective-permute-start | bytes 359432 | tf_op jit(solution)/shard_map/ppermute | solution.py:25
  42.4 12.9 %copy-start.2 = (bf16[1,512,16,256]{1,3,2,0:T(8,128)(2,1)S(1)}, bf16[1,512,16,256]{1,3,2,0:T(8,128)(2,1)}, u32[]{:S(2)}) copy-start(bf16[1,512,16,256]{1,3,2,0:T(8,128)(2,1)} %copy.200) | copy-start | bytes 12582916
  42.4 6.5 collective-permute-start.9
  46.1 4.9 collective-permute-start.3
  48.9 6.4 collective-permute-start.2
  48.9 16.4 %collective-permute-start.10 = (bf16[117,512]{1,0:T(8,128)(2,1)S(1)}, bf16[117,512]{1,0:T(8,128)(2,1)S(1)}, u32[]{:S(2)}, u32[]{:S(2)}) collective-permute-start(bf16[117,512]{1,0:T(8,128)(2,1)S(1)} %collective-permute-done.9), channel_id=1, source_target_pairs={{0,64},{64,0},{16,80},{80,16},{32,96},{96,32},{48,112},{112,48},{1... | collective-permute-start | bytes 359432 | tf_op jit(solution)/shard_map/ppermute | solution.py:15
  69.4 84.4 %collective-permute-start.13 = (bf16[117,34,1]{0,1,2:T(8,128)(2,1)S(1)}, bf16[117,34,1]{0,1,2:T(8,128)(2,1)S(1)}, u32[]{:S(2)}, u32[]{:S(2)}) collective-permute-start(bf16[117,34,1]{0,1,2:T(8,128)(2,1)S(1)} %copy.227), channel_id=1, source_target_pairs={{16,0},{32,16},{48,32},{64,48},{80,64},{96,80},{112,96},{0,112},{1... | collective-permute-start | bytes 23876 | tf_op jit(solution)/shard_map/ppermute | solution.py:27
  70.4 84.0 %collective-permute-start.12 = (bf16[117,34,1]{0,1,2:T(8,128)(2,1)S(1)}, bf16[117,34,1]{0,1,2:T(8,128)(2,1)S(1)}, u32[]{:S(2)}, u32[]{:S(2)}) collective-permute-start(bf16[117,34,1]{0,1,2:T(8,128)(2,1)S(1)} %copy.226), channel_id=1, source_target_pairs={{0,16},{16,32},{32,48},{48,64},{64,80},{80,96},{96,112},{112,0},{1... | collective-permute-start | bytes 23876 | tf_op jit(solution)/shard_map/ppermute | solution.py:25
  205.1 46.7 %copy-start.4 = (bf16[117,17,257]{2,0,1:T(8,128)(2,1)}, bf16[117,17,257]{2,0,1:T(8,128)(2,1)S(1)}, u32[]{:S(2)}) copy-start(bf16[117,17,257]{2,0,1:T(8,128)(2,1)S(1)} %slice.271) | copy-start | bytes 3067042
  392.4 293.4 %all-reduce.5.cloned.1.call-start = ((), (), s32[]{:S(2)}) async-start(), calls=%async_computation.1 | async-start | bytes 7667712 | tf_op jit(solution)/shard_map/psum | solution.py:87
  526.7 82.4 %collective-permute-start.4 = (bf16[117,512]{0,1:T(8,128)(2,1)S(1)}, bf16[117,512]{0,1:T(8,128)(2,1)S(1)}, u32[]{:S(2)}, u32[]{:S(2)}) collective-permute-start(bf16[117,512]{0,1:T(8,128)(2,1)S(1)} %convert_element_type.45), channel_id=1, source_target_pairs={{0,16},{16,0},{32,48},{48,32},{64,80},{80,64},{96,112},{112,96},{1... | collective-permute-start | bytes 359432 | tf_op jit(solution)/shard_map/ppermute | solution.py:15
  609.0 9.4 %copy-start.11 = (bf16[117,16,256,1]{0,2,1,3:T(8,128)(2,1)S(1)}, bf16[117,16,256,1]{0,2,1,3:T(8,128)(2,1)}, u32[]{:S(2)}) copy-start(bf16[117,16,256,1]{0,2,1,3:T(8,128)(2,1)} %get-tuple-element.80) | copy-start | bytes 2875396
  609.0 7.1 %collective-permute-start.5 = (bf16[117,512]{0,1:T(8,128)(2,1)S(1)}, bf16[117,512]{0,1:T(8,128)(2,1)S(1)}, u32[]{:S(2)}, u32[]{:S(2)}) collective-permute-start(bf16[117,512]{0,1:T(8,128)(2,1)S(1)} %collective-permute-done.4), channel_id=1, source_target_pairs={{0,32},{32,0},{16,48},{48,16},{64,96},{96,64},{80,112},{112,80},{1... | collective-permute-start | bytes 359432 | tf_op jit(solution)/shard_map/ppermute | solution.py:15
  616.1 9.0 %collective-permute-start.6 = (bf16[117,512]{0,1:T(8,128)(2,1)S(1)}, bf16[117,512]{0,1:T(8,128)(2,1)S(1)}, u32[]{:S(2)}, u32[]{:S(2)}) collective-permute-start(bf16[117,512]{0,1:T(8,128)(2,1)S(1)} %collective-permute-done.5), channel_id=1, source_target_pairs={{0,64},{64,0},{16,80},{80,16},{32,96},{96,32},{48,112},{112,48},{1... | collective-permute-start | bytes 359432 | tf_op jit(solution)/shard_map/ppermute | solution.py:15
  618.4 10.1 %copy-start.18 = (f32[16,256]{1,0:T(8,128)S(1)}, f32[16,256]{1,0:T(8,128)}, u32[]{:S(2)}) copy-start(f32[16,256]{1,0:T(8,128)} %slice.257) | copy-start | bytes 49156
  618.4 10.1 %copy-start.19 = (f32[16,256]{1,0:T(8,128)S(1)}, f32[16,256]{1,0:T(8,128)}, u32[]{:S(2)}) copy-start(f32[16,256]{1,0:T(8,128)} %slice.264) | copy-start | bytes 49156
  (15 other events, 52.7 us)
Sparse Core Ops, SparseCore 0:
  392.5 106.0 all-reduce.2
  501.1 184.5 all-reduce.4
